TPU v7x, 512 devices: a whole 4x4x16 slice. The times are simulated.
512 devices in a mesh: rowg: 16 (over y_hi, x, core), colg: 32 (over y_lo, z).
Axes of the slice: x: 4, y: 4 (y_hi: 2, y_lo: 2; y = y_hi * 2 + y_lo), z: 16, core: 2. Of those that a mesh axis runs over, the one named last changes fastest.
Arguments:
- pair_rows: int32 [8192, 32768], P('rowg', 'colg'), may hold values from 0 to 240
- reducers: int32 [2, 1024, 32768], P(None, 'rowg', 'colg'), may hold values from 0 to 240
- pivots: int32 [2, 1024], replicated, may hold values from 0 to 32767, as said below
- counts: int32 [16], replicated, may hold values from 0 to 512, as said below
Outputs:
- reduced: int32 [4096, 32768], P('rowg', 'colg')
Inputs may be any that keep to these rules, and one draw needn't show every extreme that they name: `pivots`: the 2048 pivot columns are all different; column 0 and column 32767 are among them. `counts`: owners 2i and 2i + 1 together hold 512 live rows; some owner has exactly 512 live rows and its partner none; owner 16 - 2 holds more than 256 live rows.
All inputs are finite; a program needn't handle non-finite values.
Results may differ from a plain program's by a relative error of at most 0.000001.
Values may be sent and summed in bfloat16 or wider, within the bound.
No kernel may reach another device: no remote copies, remote signals or barrier semaphores. Data moves between devices by JAX's collectives and lax.ppermute only.
A program may use at most 64 MiB of HBM per device.

v0:
```python
import jax
import jax.numpy as jnp
from jax import lax
from jax.sharding import Mesh, PartitionSpec as P

PANELS = 2
LIVE_DEV = 256
CAP = 96
ROW = ("yh", "x", "core")
COL = ("yl", "z")
modulus = 241.0
half_modulus = 120.0


def centered(values):
    return values - modulus * (values > half_modulus).astype(values.dtype)


def pick_value(table, position):
    marks = lax.iota(jnp.int32, table.shape[0]) == position
    return jnp.sum(jnp.where(marks, table, jnp.zeros_like(table)))


def swap(value, axis):
    return lax.ppermute(value, axis, [(0, 1), (1, 0)])


def take_window(source, start, rows):
    index = start + lax.iota(jnp.int32, rows)
    return jnp.take(source, jnp.clip(index, 0, source.shape[0] - 1), axis=0)


def compact_rows(pair_rows, counts):
    row_index = lax.axis_index(ROW)
    second = lax.axis_index("core")
    first_count = pick_value(counts, row_index - second)
    slots = pair_rows.astype(jnp.float32).astype(jnp.bfloat16)
    keep_start = second * (LIVE_DEV - first_count)
    send_start = jnp.where(second == 0, LIVE_DEV, -first_count)
    kept = take_window(slots, keep_start, LIVE_DEV)
    incoming = swap(take_window(slots, send_start, LIVE_DEV), "core")
    place = lax.iota(jnp.int32, LIVE_DEV)
    mine = jnp.where(second == 0, place < first_count, place >= first_count - LIVE_DEV)
    return jnp.where(mine[:, None], kept, incoming)


def normalize_block(block, own_cols, all_pivots, col_start):
    columns = col_start + lax.iota(jnp.int32, block.shape[1])
    is_pivot = jnp.any(columns[:, None] == all_pivots[None, :], axis=1)
    own_pivot = columns[None, :] == own_cols[:, None]
    entries = centered(block.astype(jnp.float32))
    ones = jnp.ones_like(entries)
    zeros = jnp.zeros_like(entries)
    kept = jnp.where(is_pivot[None, :], jnp.where(own_pivot, ones, zeros), entries)
    return kept.astype(jnp.bfloat16)


def shards(pair_rows, reducers, pivots, counts):
    row_index = lax.axis_index(ROW)
    col_index = lax.axis_index(COL)
    lower = lax.axis_index("yl")
    col_width = pair_rows.shape[1]
    col_start = col_index * col_width
    rows_dev = reducers.shape[1]
    order = pivots.reshape(PANELS, -1, rows_dev).transpose(1, 0, 2).reshape(-1)
    total = order.shape[0]
    own_cols = lax.dynamic_slice_in_dim(order, row_index * PANELS * rows_dev, PANELS * rows_dev)
    normed = normalize_block(
        reducers.reshape(PANELS * rows_dev, col_width), own_cols, order, col_start
    )
    panel = lax.all_gather(normed, ROW, axis=0, tiled=True)
    live = compact_rows(pair_rows, counts)
    owner = order // col_width
    ids = lax.iota(jnp.int32, total)
    same = owner[:, None] == owner[None, :]
    rank = jnp.sum((same & (ids[None, :] < ids[:, None])).astype(jnp.int32), axis=1)
    rounds = jnp.max(rank) // CAP + 1
    z_size = lax.axis_size("z")
    slot = owner % z_size * (2 * CAP) + owner // z_size * CAP

    def fetch(step):
        base = step * CAP
        want = base + lax.iota(jnp.int32, CAP)
        hit = (owner == col_index)[None, :] & (rank[None, :] == want[:, None])
        local = jnp.sum(jnp.where(hit, order[None, :] - col_start + 1, 0), axis=1) - 1
        choose = (local[:, None] == lax.iota(jnp.int32, col_width)[None, :]).astype(jnp.bfloat16)
        mine = lax.dot_general(
            choose, live, (((1,), (1,)), ((), ())), preferred_element_type=jnp.float32
        )
        mine = centered(mine).astype(jnp.bfloat16)
        theirs = swap(mine, "yl")
        both = jnp.where(lower == 0, jnp.stack([mine, theirs]), jnp.stack([theirs, mine]))
        spread = lax.all_gather(both.reshape(2 * CAP, LIVE_DEV), "z", axis=0, tiled=True)
        inside = (rank >= base) & (rank < base + CAP)
        got = jnp.take(spread, jnp.where(inside, slot + rank - base, 0), axis=0)
        return jnp.where(inside[:, None], got, jnp.zeros_like(got))

    half = total // 2

    def reduce_by(result, factors):
        for part in range(2):
            product = lax.dot_general(
                factors[part * half : (part + 1) * half],
                panel[part * half : (part + 1) * half],
                (((0,), (0,)), ((), ())),
                preferred_element_type=jnp.float32,
            )
            result = jnp.mod(result - product, modulus)
        return result

    first = reduce_by(live.astype(jnp.float32), fetch(0)).astype(jnp.int32)
    _, result = lax.while_loop(
        lambda state: state[0] < rounds,
        lambda state: (
            state[0] + 1,
            reduce_by(state[1].astype(jnp.float32), fetch(state[0])).astype(jnp.int32),
        ),
        (jnp.int32(1), first),
    )
    return result


def solution(mesh):
    fine = Mesh(mesh.devices.reshape(2, 4, 2, 2, 16), (*ROW, *COL))
    return jax.shard_map(
        shards,
        mesh=fine,
        in_specs=(P(ROW, COL), P(None, ROW, COL), P(), P()),
        out_specs=P(ROW, COL),
        check_vma=False,
    )
```

profile of v0, /device:TPU:1, one launch (start us, length us, event | category | flops | bytes accessed | tf_op | source)
XLA Modules:
  0.0 193.9 jit_solution(13259388793298008587)
XLA Ops:
  6.5 0.0 all-gather.4.cloned.1.call-start
  6.5 1.3 fusion.55
  8.5 0.0 copy-start.4
  8.5 1.8 convert_convert_fusion
  10.4 1.2 gather_fusion.3
  11.6 0.0 copy-start.2
  11.6 0.1 broadcast_select_fusion
  11.7 8.9 %collective-permute-start.1 = (bf16[256,1024]{1,0:T(8,128)(2,1)S(1)}, bf16[256,1024]{1,0:T(8,128)(2,1)S(1)}, u32[]{:S(2)}, u32[]{:S(2)}) collective-permute-start(bf16[256,1024]{1,0:T(8,128)(2,1)S(1)} %broadcast_select_fusion), channel_id=1, source_target_pairs={{0,32},{32,0},{1,33},{33,1},{2,34},{34,2},{3,35},{35,3},{4,36},{36... | collective-permute-start | bytes 1572872 | tf_op jit(solution)/shard_map/ppermute | solution.py:25
  21.3 0.0 copy-done.4
  21.3 0.1 reshape.383
  21.4 0.1 reshape.384
  21.5 4.5 %convert_reduce_fusion = s32[2048]{0:T(1024)S(1)} fusion(s32[2048]{0:T(1024)S(1)} %get-tuple-element.336), kind=kLoop, calls=%fused_computation.34 | loop fusion | flops 20969472 | bytes 16384 | tf_op jit(solution)/shard_map/reduce_sum | solution.py:76
  26.6 1.2 gather_fusion.2
  27.8 0.7 compare_and_fusion.5
  28.4 0.3 select_reduce_fusion.1
  28.7 0.0 collective-permute-done.1
  28.7 0.0 copy-start.3
  28.7 0.8 copy-done.3
  29.5 1.2 select_select_fusion.2
  30.7 0.3 subtract_convert_fusion.1
  31.0 1.9 collective-permute-start.2
  33.0 3.2 %collective-permute-done.2 = bf16[96,256]{1,0:T(8,128)(2,1)S(1)} collective-permute-done((bf16[96,256]{1,0:T(8,128)(2,1)S(1)}, bf16[96,256]{1,0:T(8,128)(2,1)S(1)}, u32[]{:S(2)}, u32[]{:S(2)}) %collective-permute-start.2) | collective-permute-done | bytes 49184 | tf_op jit(solution)/shard_map/ppermute | solution.py:25
  36.2 0.6 maximum_select_fusion.1
  36.9 0.0 all-gather.4.cloned.1.call-update
  36.9 0.0 all-gather.6.cloned.1.call-start
  36.9 0.1 dynamic_slice.3
  37.0 1.2 compare_reduce_fusion
  38.2 0.0 copy-done.2
  38.2 0.8 fusion.39
  39.0 0.0 all-gather.6.cloned.1.call-update
  39.1 0.7 reduce_max.9
  41.6 0.1 reshape.385
  41.7 0.1 compare_select_fusion.2
  41.8 56.7 %all-gather.4.cloned.1.call-done = bf16[3072,256]{1,0:T(8,128)(2,1)} async-done(((bf16[192,256]{1,0:T(8,128)(2,1)}), bf16[3072,256]{1,0:T(8,128)(2,1)}) %all-gather.4.cloned.1.call-update) | async-done | bytes 1572880 | tf_op jit(solution)/shard_map/all_gather | solution.py:93
  98.6 8.2 %gather_fusion.1 = bf16[2048,256]{1,0:T(8,128)(2,1)S(1)} fusion(bf16[3072,256]{1,0:T(8,128)(2,1)} %all-gather.4.cloned.1.call-done, s32[2048]{0:T(1024)S(1)} %broadcast_clamp_fusion.1), kind=kCustom, calls=%fused_computation.3 | custom fusion | bytes 2105344 | tf_op jit(solution)/shard_map/jit(_take)/gather | solution.py:95
  106.8 1.5 select_select_fusion.1
  108.3 72.3 %all-gather.6.cloned.1.call-done = bf16[2048,1024]{1,0:T(8,128)(2,1)} async-done(((bf16[128,1024]{1,0:T(8,128)(2,1)}), bf16[2048,1024]{1,0:T(8,128)(2,1)}) %all-gather.6.cloned.1.call-update) | async-done | bytes 4194320 | tf_op jit(solution)/shard_map/all_gather | solution.py:71
  180.6 2.3 %fusion.26 = f32[256,1024]{1,0:T(8,128)S(1)} fusion(bf16[2048,1024]{1,0:T(8,128)(2,1)} %all-gather.6.cloned.1.call-done, bf16[2048,256]{1,0:T(8,128)(2,1)S(1)} %select_select_fusion.1), kind=kOutput, calls=%fused_computation.40 | convolution fusion | flops 536870912 | bytes 3670016 | tf_op jit(solution)/shard_map/dot_general | solution.py:102
  183.0 3.1 %fusion.30 = s32[256,1024]{1,0:T(8,128)S(1)} fusion(f32[256,1024]{1,0:T(8,128)S(1)} %fusion.26, bf16[256,1024]{1,0:T(8,128)(2,1)S(1)} %select_select_fusion.2, bf16[2048,1024]{1,0:T(8,128)(2,1)} %all-gather.6.cloned.1.call-done, bf16[2048,256]{1,0:T(8,128)(2,1)S(1)} %select_select_fusion.1), kind=kOutput, calls=%fused_computation.47 | convolution fusion | flops 541065216 | bytes 5242880 | tf_op jit(solution)/shard_map/dot_general | solution.py:102
  186.1 0.0 copy-start.1
  186.1 1.0 copy-done.1
  (13 shorter events, 0.1 us)
Async XLA Ops:
  6.5 92.0 %all-gather.4.cloned.1.call-start = ((), (), s32[]{:S(2)}) async-start(), calls=%async_computation | async-start | bytes 1671168 | tf_op jit(solution)/shard_map/all_gather | solution.py:93
  8.5 12.7 %copy-start.4 = (s32[2,1024]{1,0:T(2,128)S(1)}, s32[2,1024]{1,0:T(2,128)}, u32[]{:S(2)}) copy-start(s32[2,1024]{1,0:T(2,128)} %param.10) | copy-start | bytes 24580
  11.6 26.6 %copy-start.2 = (s32[2,64,1024]{2,1,0:T(8,128)S(1)}, s32[2,64,1024]{2,1,0:T(8,128)}, u32[]{:S(2)}) copy-start(s32[2,64,1024]{2,1,0:T(8,128)} %param.9) | copy-start | bytes 1572868
  11.7 17.0 %collective-permute-start.1 = (bf16[256,1024]{1,0:T(8,128)(2,1)S(1)}, bf16[256,1024]{1,0:T(8,128)(2,1)S(1)}, u32[]{:S(2)}, u32[]{:S(2)}) collective-permute-start(bf16[256,1024]{1,0:T(8,128)(2,1)S(1)} %broadcast_select_fusion), channel_id=1, source_target_pairs={{0,32},{32,0},{1,33},{33,1},{2,34},{34,2},{3,35},{35,3},{4,36},{36... | collective-permute-start | bytes 1572872 | tf_op jit(solution)/shard_map/ppermute | solution.py:25
  28.7 0.8 copy-start.3
  31.0 5.2 %collective-permute-start.2 = (bf16[96,256]{1,0:T(8,128)(2,1)S(1)}, bf16[96,256]{1,0:T(8,128)(2,1)S(1)}, u32[]{:S(2)}, u32[]{:S(2)}) collective-permute-start(bf16[96,256]{1,0:T(8,128)(2,1)S(1)} %subtract_convert_fusion.1), channel_id=1, source_target_pairs={{0,16},{16,0},{1,17},{17,1},{2,18},{18,2},{3,19},{19,3},{4,20},{20... | collective-permute-start | bytes 147464 | tf_op jit(solution)/shard_map/ppermute | solution.py:25
  36.9 143.8 %all-gather.6.cloned.1.call-start = ((), (), s32[]{:S(2)}) async-start(), calls=%async_computation.1 | async-start | bytes 4456448 | tf_op jit(solution)/shard_map/all_gather | solution.py:71
  186.1 1.0 copy-start.1
Sparse Core Ops, SparseCore 0:
  37.0 61.5 all-gather.3
  101.9 78.7 all-gather.5
where the time goes:
time: 194 us
  waiting for transfers between devices  132 us (68%)
  between operations  17.4 us (9%)
  other arithmetic  14.9 us (8%)
  local copies, waits for them, and re-layouts  12.7 us (7%)
  starting transfers between devices  10.8 us (6%)
  matrix products  5.73 us (3%)
    all_gather x1, waiting for transfers between devices, shards(): panel = lax.all_gather(normed, ROW, axis=0, tiled=True)  72.3 us
    all_gather x1, waiting for transfers between devices, fetch(): lax.all_gather(both.reshape(2 * CAP, LIVE_DEV), 'z', axis=0, tiled=True)  56.7 us
    ppermute x2, starting transfers between devices, swap(): return lax.ppermute(value, axis, [(0, 1), (1, 0)])  10.8 us
    gather x1, local copies, waits for them, and re-layouts, fetch(): got = jnp.take(spread, jnp.where(inside, slot + rank - base, 0), axis=0)  8.24 us
    dot_general x2, matrix products, reduce_by(): lax.dot_general(factors[part * half:(part + 1) * half], panel[part * half...  5.42 us
    reduce_sum x1, other arithmetic, shards(): jnp.sum((same & (ids[None, :] < ids[:, None])).astype(jnp.int32), axis=1)  4.48 us
  transfers between devices with their start and end apart: 4, of which 3 were waited for; matrix products, arithmetic and copies ran while one was open for 10% of the time, Pallas kernels for 0%

commit v1 on v0

--- a/solution.py
+++ b/solution.py
@@ -10,6 +10,18 @@
 COL = ("yl", "z")
 modulus = 241.0
 half_modulus = 120.0
+
+
+def use_shapes_now(which_dim, inp):
+    return jnp.concatenate(
+        lax.all_to_all(
+            jnp.stack([inp for _ in range(lax.axis_size(ROW))], axis=0),
+            split_axis=0,
+            axis_name=ROW,
+            concat_axis=0,
+        ),
+        axis=which_dim,
+    )
 
 
 def centered(values):
@@ -68,7 +80,7 @@
     normed = normalize_block(
         reducers.reshape(PANELS * rows_dev, col_width), own_cols, order, col_start
     )
-    panel = lax.all_gather(normed, ROW, axis=0, tiled=True)
+    panel = use_shapes_now(0, normed)
     live = compact_rows(pair_rows, counts)
     owner = order // col_width
     ids = lax.iota(jnp.int32, total)

time: 194 us -> 174 us (0.90)
  the two profiles are of different devices: /device:TPU:1 before, /device:TPU:8 now
where the time goes in v1:
time: 174 us; the launch traced here: 173 us
  waiting for transfers between devices  108 us (62%)
  between operations  17.5 us (10%)
  local copies, waits for them, and re-layouts  17.1 us (10%)
  starting transfers between devices  14.2 us (8%)
  other arithmetic  13.1 us (8%)
  matrix products  2.75 us (2%)
    all_gather x1, waiting for transfers between devices, fetch(): lax.all_gather(both.reshape(2 * CAP, LIVE_DEV), 'z', axis=0, tiled=True)  76.6 us
    ppermute x2, waiting for transfers between devices, swap(): return lax.ppermute(value, axis, [(0, 1), (1, 0)])  31.9 us
    gather x1, local copies, waits for them, and re-layouts, fetch(): got = jnp.take(spread, jnp.where(inside, slot + rank - base, 0), axis=0)  8.25 us
    ppermute x2, starting transfers between devices, swap(): return lax.ppermute(value, axis, [(0, 1), (1, 0)])  7.87 us
    all_to_all x1, starting transfers between devices, use_shapes_now(): lax.all_to_all(jnp.stack([inp for _ in range(lax.axis_size(ROW))], axis=0...  6.29 us
    reduce_sum x1, other arithmetic, shards(): jnp.sum((same & (ids[None, :] < ids[:, None])).astype(jnp.int32), axis=1)  4.48 us
  transfers between devices with their start and end apart: 4, of which 2 were waited for; matrix products, arithmetic and copies ran while one was open for 13% of the time, Pallas kernels for 0%

profile of v1, /device:TPU:8, one launch (start us, length us, event | category | flops | bytes accessed | tf_op | source)
XLA Modules:
  0.0 173.3 jit_solution(5725031537456044209)
XLA Ops:
  6.5 1.3 fusion.51
  8.5 1.8 %convert_convert_fusion = bf16[512,1024]{1,0:T(8,128)(2,1)S(1)} fusion(s32[512,1024]{1,0:T(8,128)} %param.8), kind=kLoop, calls=%fused_computation.38 | loop fusion | flops 1048576 | bytes 3145728 | tf_op jit(solution)/shard_map/convert_element_type | solution.py:49
  10.4 0.0 copy-start.2
  10.4 0.0 copy-start.1
  10.4 1.2 gather_fusion.3
  11.6 0.1 broadcast_select_fusion
  11.7 1.9 %collective-permute-start.1 = (bf16[256,1024]{1,0:T(8,128)(2,1)S(1)}, bf16[256,1024]{1,0:T(8,128)(2,1)S(1)}, u32[]{:S(2)}, u32[]{:S(2)}) collective-permute-start(bf16[256,1024]{1,0:T(8,128)(2,1)S(1)} %broadcast_select_fusion), channel_id=1, source_target_pairs={{0,32},{32,0},{1,33},{33,1},{2,34},{34,2},{3,35},{35,3},{4,36},{36... | collective-permute-start | bytes 1572872 | tf_op jit(solution)/shard_map/ppermute | solution.py:37
  13.6 0.0 copy-done.2
  13.6 0.1 reshape.416
  13.7 0.1 reshape.417
  13.8 0.1 dynamic_slice.3
  13.9 1.2 compare_reduce_fusion
  15.1 0.0 copy-done.1
  15.1 0.1 fusion.35
  15.2 2.5 %stack.63 = bf16[16,128,1024]{2,1,0:T(8,128)(2,1)} broadcast(bf16[128,1024]{1,0:T(8,128)(2,1)S(1)} %fusion.35), dimensions={1,2} | broadcast | bytes 4456448 | tf_op jit(solution)/shard_map/stack | solution.py:18
  17.7 6.3 %all-to-all-start = ((bf16[16,128,1024]{2,1,0:T(8,128)(2,1)}), bf16[16,128,1024]{2,1,0:T(8,128)(2,1)}, u32[]{:S(2)}, u32[]{:S(2)}) async-start(bf16[16,128,1024]{2,1,0:T(8,128)(2,1)} %stack.63), calls=%async_computation | async-start | bytes 8388608 | tf_op jit(solution)/shard_map/all_to_all | solution.py:17
  24.0 0.0 all-gather.3.cloned.1.call-start
  24.8 4.5 %convert_reduce_fusion = s32[2048]{0:T(1024)S(1)} fusion(s32[2048]{0:T(1024)S(1)} %get-tuple-element.338), kind=kLoop, calls=%fused_computation.34 | loop fusion | flops 20969472 | bytes 16384 | tf_op jit(solution)/shard_map/reduce_sum | solution.py:88
  29.9 1.2 gather_fusion.2
  31.1 0.7 compare_and_fusion.5
  31.7 0.3 select_reduce_fusion.1
  32.0 0.0 collective-permute-done.1
  32.0 0.1 select_select_fusion.2
  32.2 0.3 subtract_convert_fusion.1
  32.5 5.9 %collective-permute-start.2 = (bf16[96,256]{1,0:T(8,128)(2,1)S(1)}, bf16[96,256]{1,0:T(8,128)(2,1)S(1)}, u32[]{:S(2)}, u32[]{:S(2)}) collective-permute-start(bf16[96,256]{1,0:T(8,128)(2,1)S(1)} %subtract_convert_fusion.1), channel_id=1, source_target_pairs={{0,16},{16,0},{1,17},{17,1},{2,18},{18,2},{3,19},{19,3},{4,20},{20... | collective-permute-start | bytes 147464 | tf_op jit(solution)/shard_map/ppermute | solution.py:37
  38.4 31.9 %collective-permute-done.2 = bf16[96,256]{1,0:T(8,128)(2,1)S(1)} collective-permute-done((bf16[96,256]{1,0:T(8,128)(2,1)S(1)}, bf16[96,256]{1,0:T(8,128)(2,1)S(1)}, u32[]{:S(2)}, u32[]{:S(2)}) %collective-permute-start.2) | collective-permute-done | bytes 49184 | tf_op jit(solution)/shard_map/ppermute | solution.py:37
  70.3 0.7 maximum_select_fusion.1
  70.9 0.0 all-gather.3.cloned.1.call-update
  71.0 0.1 reshape.418
  71.1 0.7 reduce_max.9
  73.6 0.1 compare_select_fusion.2
  73.8 76.6 %all-gather.3.cloned.1.call-done = bf16[3072,256]{1,0:T(8,128)(2,1)} async-done(((bf16[192,256]{1,0:T(8,128)(2,1)}), bf16[3072,256]{1,0:T(8,128)(2,1)}) %all-gather.3.cloned.1.call-update) | async-done | bytes 1572880 | tf_op jit(solution)/shard_map/all_gather | solution.py:105
  150.4 8.2 %gather_fusion.1 = bf16[2048,256]{1,0:T(8,128)(2,1)S(1)} fusion(bf16[3072,256]{1,0:T(8,128)(2,1)} %all-gather.3.cloned.1.call-done, s32[2048]{0:T(1024)S(1)} %broadcast_clamp_fusion.1), kind=kCustom, calls=%fused_computation.3 | custom fusion | bytes 2105344 | tf_op jit(solution)/shard_map/jit(_take)/gather | solution.py:107
  158.6 1.5 select_select_fusion.1
  160.1 0.0 all-to-all-done
  160.1 2.7 %fusion.54 = (bf16[8,128,1024]{2,1,0:T(8,128)(2,1)S(1)}, bf16[8,128,1024]{2,1,0:T(8,128)(2,1)S(1)}) fusion(bf16[16,128,1024]{2,1,0:T(8,128)(2,1)} %all-to-all-done), kind=kLoop, calls=%fused_computation.116 | loop fusion | bytes 8388608 | tf_op jit(solution)/shard_map/slice | solution.py:116
  162.8 0.7 fusion.32
  163.6 1.7 fusion.26
  165.3 0.2 while.12
  165.5 0.0 copy-start
  165.5 1.0 copy-done
  (12 shorter events, 0.1 us)
Async XLA Ops:
  10.4 3.3 %copy-start.2 = (s32[2,1024]{1,0:T(2,128)S(1)}, s32[2,1024]{1,0:T(2,128)}, u32[]{:S(2)}) copy-start(s32[2,1024]{1,0:T(2,128)} %param.10) | copy-start | bytes 24580
  10.4 4.7 %copy-start.1 = (s32[2,64,1024]{2,1,0:T(8,128)S(1)}, s32[2,64,1024]{2,1,0:T(8,128)}, u32[]{:S(2)}) copy-start(s32[2,64,1024]{2,1,0:T(8,128)} %param.9) | copy-start | bytes 1572868
  11.7 20.3 %collective-permute-start.1 = (bf16[256,1024]{1,0:T(8,128)(2,1)S(1)}, bf16[256,1024]{1,0:T(8,128)(2,1)S(1)}, u32[]{:S(2)}, u32[]{:S(2)}) collective-permute-start(bf16[256,1024]{1,0:T(8,128)(2,1)S(1)} %broadcast_select_fusion), channel_id=1, source_target_pairs={{0,32},{32,0},{1,33},{33,1},{2,34},{34,2},{3,35},{35,3},{4,36},{36... | collective-permute-start | bytes 1572872 | tf_op jit(solution)/shard_map/ppermute | solution.py:37
  17.7 142.4 %all-to-all-start = ((bf16[16,128,1024]{2,1,0:T(8,128)(2,1)}), bf16[16,128,1024]{2,1,0:T(8,128)(2,1)}, u32[]{:S(2)}, u32[]{:S(2)}) async-start(bf16[16,128,1024]{2,1,0:T(8,128)(2,1)} %stack.63), calls=%async_computation | async-start | bytes 8388608 | tf_op jit(solution)/shard_map/all_to_all | solution.py:17
  24.0 126.4 %all-gather.3.cloned.1.call-start = ((), (), s32[]{:S(2)}) async-start(), calls=%async_computation.1 | async-start | bytes 1671168 | tf_op jit(solution)/shard_map/all_gather | solution.py:105
  32.5 37.8 %collective-permute-start.2 = (bf16[96,256]{1,0:T(8,128)(2,1)S(1)}, bf16[96,256]{1,0:T(8,128)(2,1)S(1)}, u32[]{:S(2)}, u32[]{:S(2)}) collective-permute-start(bf16[96,256]{1,0:T(8,128)(2,1)S(1)} %subtract_convert_fusion.1), channel_id=1, source_target_pairs={{0,16},{16,0},{1,17},{17,1},{2,18},{18,2},{3,19},{19,3},{4,20},{20... | collective-permute-start | bytes 147464 | tf_op jit(solution)/shard_map/ppermute | solution.py:37
  165.5 1.0 copy-start
Sparse Core Ops, SparseCore 0:
  71.1 79.2 all-gather.2
